TPU v7x, 32 devices: a whole 2x2x4 slice. The times are simulated.
32 devices in a mesh: row: 8 (over z, x), col: 4 (over y, core).
Axes of the slice: x: 2, y: 2, z: 4, core: 2. Of those that a mesh axis runs over, the one named last changes fastest.
Arguments:
- replica_weights: float32 [8, 4, 128, 2048], P('row', 'col'), may hold values from -4.5 to 4.5
- replica_first: float32 [8, 4, 128, 2048], P('row', 'col'), may hold values from -3.9 to 3.9
- replica_second: float32 [8, 4, 128, 2048], P('row', 'col'), may hold values from 0.05 to 8
- replica_grads: float32 [8, 4, 128, 2048], P('row', 'col'), may hold values from -9 to 9
Outputs:
- mean_weights: float32 [128, 2048], replicated
- mean_first: float32 [128, 2048], replicated
- mean_second: float32 [128, 2048], replicated
All inputs are finite; a program needn't handle non-finite values.
Results may differ from a plain program's by a relative error of at most 0.00002.
Values sent between devices are 32-bit elements; how exact they have to be, the bound alone decides.
A program may use at most 64 MiB of HBM per device.

v0:
```python
import functools

import jax
import jax.numpy as jnp
from jax import lax
from jax.experimental import pallas as pl
from jax.experimental.pallas import tpu as pltpu
from jax.sharding import PartitionSpec as P

bias_one = 0.9999734386011124
bias_two = 0.994079470779666
MESH = pl.DeviceIdType.MESH
GROUP = 16


PATTERN = "xyzyx"
SLANT = 0.1


def stage_orders(rows, cols):
    row_bits = [("row", b) for b in range((rows - 1).bit_length())]
    col_bits = [("col", b) for b in range((cols - 1).bit_length())]
    core, ys, xs, zs = col_bits[0], col_bits[1:], row_bits[0], row_bits[1:]
    single = lambda bits: [(bit,) for bit in bits]
    return {
        "x": [(core,), (xs,), *single(ys), tuple(zs)],
        "y": [(core,), *single(ys), (xs,), tuple(zs)],
        "X": [(core,), (xs,), *single(ys), *single(zs)],
        "Y": [(core,), *single(ys), (xs,), *single(zs)],
        "z": [(core,), *single(zs), (xs, *ys)],
        "d": [(core,), (xs, *ys), tuple(zs)],
        "w": [(core,), tuple(zs), (xs, *ys)],
        "a": [(core,), (xs,), tuple(zs), tuple(ys)],
        "b": [(core,), tuple(ys), tuple(zs), (xs,)],
    }


def flips(stage, m):
    return tuple(bit for j, bit in enumerate(stage) if m >> j & 1)


def plan(tiles, orders, devices):
    pieces, events = [], []
    for first in range(0, tiles, devices):
        for array in range(3):
            pieces.append((array, first, devices, PATTERN[len(pieces) % len(PATTERN)]))
    keyed = [(SLANT * p - 1, p, "compute") for p in range(0, len(pieces), 3)]
    for p, piece in enumerate(pieces):
        keyed += [(SLANT * p + k, p, k) for k in range(2 * len(orders[piece[3]]))]
    keyed.sort(key=lambda entry: entry[:2])
    for _, p, k in keyed:
        events.append(("compute", pieces[p][1]) if k == "compute" else (p, k))
    return pieces, events


def for_groups(count, body):
    if count <= GROUP:
        body(0, count)
    else:
        def step(i, carry):
            body(i * GROUP, GROUP)
            return carry

        lax.fori_loop(0, count // GROUP, step, 0)


def kernel(rows, cols, orders, pieces, events, w_hbm, f_hbm, s_hbm, g_hbm, ow, of, os, ins, acc, got, in_sem, send_sem, recv_sem):
    me = {"row": lax.axis_index("row"), "col": lax.axis_index("col")}
    outs = (ow, of, os)
    every_bit = sorted({bit for stage in orders["x"] for bit in stage})
    value = {bit: lax.rem(me[bit[0]] // (2 ** bit[1]), 2) for bit in every_bit}

    def peer(bits):
        other = dict(me)
        for bit in bits:
            other[bit[0]] = other[bit[0]] + (1 - 2 * value[bit]) * (2 ** bit[1])
        return other["row"], other["col"]

    spans = sorted({(first, count) for _, first, count, _ in pieces})
    counts = dict(spans)
    loads = {}
    for i, (first, count) in enumerate(spans):
        for k, src in enumerate((w_hbm, f_hbm, s_hbm, g_hbm)):
            loads[first, k] = pltpu.make_async_copy(
                src.at[pl.ds(first, count)], ins.at[k, pl.ds(first, count)], in_sem.at[k, i]
            )
            loads[first, k].start()

    used = {piece[3] for piece in pieces}
    met = sorted({flips(st, m) for o in used for st in orders[o] for m in range(1, 1 << len(st))})
    barrier = pltpu.get_barrier_semaphore()
    for bits in met:
        pl.semaphore_signal(barrier, inc=1, device_id=peer(bits), device_id_type=MESH)
    entered = []

    part, size, slot = {}, {}, {}
    slots = 0
    for p, (array, first, count, order) in enumerate(pieces):
        off, n = first, count
        for s, stage in enumerate(orders[order]):
            n >>= len(stage)
            size[p, s] = n
            for m in range(1 << len(stage)):
                at = off
                for j, bit in enumerate(stage):
                    v = value[bit]
                    at = at + (1 - v if m >> j & 1 else v) * (n << j)
                part[p, s, m] = at
                if m:
                    slot[p, s, m] = slots
                    slots += 2
            off = part[p, s, 0]

    def reduce_copy(p, s, m):
        array, n = pieces[p][0], size[p, s]
        return pltpu.make_async_remote_copy(
            src_ref=acc.at[array, pl.ds(part[p, s, m], n)],
            dst_ref=got.at[array, pl.ds(part[p, s, 0], n)],
            send_sem=send_sem.at[slot[p, s, m]],
            recv_sem=recv_sem.at[slot[p, s, m]],
            device_id=peer(flips(orders[pieces[p][3]][s], m)),
            device_id_type=MESH,
        )

    def gather_copy(p, s, m):
        here = outs[pieces[p][0]].at[pl.ds(part[p, s, 0], size[p, s])]
        return pltpu.make_async_remote_copy(
            src_ref=here,
            dst_ref=here,
            send_sem=send_sem.at[slot[p, s, m] + 1],
            recv_sem=recv_sem.at[slot[p, s, m] + 1],
            device_id=peer(flips(orders[pieces[p][3]][s], m)),
            device_id_type=MESH,
        )

    def others(p, s):
        return range(1, 1 << len(orders[pieces[p][3]][s]))

    copies = []

    def go(copy):
        copy.start()
        copies.append(copy)

    def total(p, s, at, n):
        array = pieces[p][0]
        shift = at - part[p, s, 0]
        value = acc[array, pl.ds(at, n)]
        for m in others(p, s):
            value = value + got[array, pl.ds(part[p, s, m] + shift, n)]
        return value

    def add(p, s, at, n):
        def body(i, m):
            acc[pieces[p][0], pl.ds(at + i, m)] = total(p, s, at + i, m)

        for_groups(n, body)

    def adamw(first, count):
        def body(i, m):
            here = pl.ds(first + i, m)
            old, grad = ins[0, here], ins[3, here]
            new_first = 0.9 * ins[1, here] + 0.1 * grad
            new_second = 0.95 * ins[2, here] + 0.05 * grad * grad
            update = (new_first * (1.0 / bias_one)) / (
                jnp.sqrt(new_second * (1.0 / bias_two)) + 1e-08
            ) + 0.1 * old
            acc[0, here] = old - 0.003 * update
            acc[1, here] = new_first
            acc[2, here] = new_second

        for_groups(count, body)

    scale = 1.0 / (rows * cols)
    for p, k in events:
        if p == "compute":
            for j in range(4):
                loads[k, j].wait()
            adamw(k, counts[k])
            if not entered:
                pl.semaphore_wait(barrier, len(met))
                entered.append(True)
            for q, piece in enumerate(pieces):
                if piece[1] == k:
                    for m in others(q, 0):
                        go(reduce_copy(q, 0, m))
            continue
        steps = len(orders[pieces[p][3]])
        s = k if k < steps else 2 * steps - 1 - k
        for m in others(p, s):
            (reduce_copy if k < steps else gather_copy)(p, s, m).wait_recv()
        if k + 1 < steps:
            n = size[p, s + 1]
            for m in others(p, s + 1):
                add(p, s, part[p, s + 1, m], n)
                go(reduce_copy(p, s + 1, m))
            add(p, s, part[p, s + 1, 0], n)
        elif k + 1 == steps:
            at, n = part[p, s, 0], size[p, s]
            outs[pieces[p][0]][pl.ds(at, n)] = total(p, s, at, n) * scale
            for m in others(p, s):
                go(gather_copy(p, s, m))
        elif s > 0:
            for m in others(p, s - 1):
                go(gather_copy(p, s - 1, m))
    for copy in copies:
        copy.wait_send()


def as_tiles(x):
    r, c = x.shape
    return x.reshape(r // 8, 8, c // 128, 128).transpose(0, 2, 1, 3).reshape(r * c // 1024, 8, 128)


def from_tiles(x, shape):
    r, c = shape
    return x.reshape(r // 8, c // 128, 8, 128).transpose(0, 2, 1, 3).reshape(r, c)


def solution(mesh):
    rows, cols = mesh.shape["row"], mesh.shape["col"]

    def on_device(*arrays):
        shape = arrays[0].shape[2:]
        tiles = shape[0] * shape[1] // 1024
        orders = stage_orders(rows, cols)
        pieces, events = plan(tiles, orders, rows * cols)
        slots = sum(2 * ((1 << len(stage)) - 1) for piece in pieces for stage in orders[piece[3]])
        spans = len({piece[1] for piece in pieces})
        result = pl.pallas_call(
            functools.partial(kernel, rows, cols, orders, pieces, events),
            out_shape=(pltpu.VMEM((tiles, 8, 128), jnp.float32),) * 3,
            in_specs=[pl.BlockSpec(memory_space=pltpu.HBM)] * 4,
            out_specs=(pl.BlockSpec(memory_space=pltpu.VMEM),) * 3,
            scratch_shapes=[
                pltpu.VMEM((4, tiles, 8, 128), jnp.float32),
                pltpu.VMEM((3, tiles, 8, 128), jnp.float32),
                pltpu.VMEM((3, tiles, 8, 128), jnp.float32),
                pltpu.SemaphoreType.DMA((4, spans)),
                pltpu.SemaphoreType.DMA((slots,)),
                pltpu.SemaphoreType.DMA((slots,)),
            ],
            compiler_params=pltpu.CompilerParams(
                collective_id=0, has_side_effects=True, vmem_limit_bytes=48 * 1024 * 1024
            ),
        )(*(pltpu.with_memory_space_constraint(as_tiles(x[0, 0]), pltpu.HBM) for x in arrays))
        return tuple(from_tiles(x, shape) for x in result)

    in_specs = (P("row", "col", None, None),) * 4
    return jax.shard_map(
        on_device, mesh=mesh, in_specs=in_specs, out_specs=(P(), P(), P()), check_vma=False
    )
```

profile of v0, /device:TPU:0, one launch (start us, length us, event | category | flops | bytes accessed | tf_op | source)
XLA Modules:
  0.0 49.9 jit_solution(14586131794629252768)
XLA Ops:
  0.6 46.4 %shard_map.67 = (f32[256,8,128]{2,1,0:T(8,128)S(1)}, f32[256,8,128]{2,1,0:T(8,128)S(1)}, f32[256,8,128]{2,1,0:T(8,128)S(1)}) custom-call(f32[256,8,128]{2,1,0:T(8,128)} %bitcast.38, f32[256,8,128]{2,1,0:T(8,128)} %bitcast.39, f32[256,8,128]{2,1,0:T(8,128)} %bitcast.40, f32[256,8,128]{2,1,0:T(8,128)} %bitcast.41), custom_call_target="tpu_custom_call" | custom-call | tf_op jit(solution)/shard_map/pallas_call | solution.py:230
  47.0 1.0 %copy.10 = f32[128,2048]{1,0:T(8,128)} copy(f32[128,2048]{1,0:T(8,128)S(1)} %bitcast.37) | data formatting | bytes 2097152
  48.0 1.0 %copy.11 = f32[128,2048]{1,0:T(8,128)} copy(f32[128,2048]{1,0:T(8,128)S(1)} %bitcast.36) | data formatting | bytes 2097152
  49.0 1.0 %copy.12 = f32[128,2048]{1,0:T(8,128)} copy(f32[128,2048]{1,0:T(8,128)S(1)} %bitcast.35) | data formatting | bytes 2097152
where the time goes:
time: 50.4 us; the launch traced here: 49.9 us
  Pallas kernels  46.4 us (92%)
  local copies, waits for them, and re-layouts  2.91 us (6%)
  between operations  0.64 us (1%)
    pallas_call x1, Pallas kernels, on_device(): pl.pallas_call(functools.partial(kernel, rows, cols, orders, pieces, even...  46.4 us
    unnamed x3, local copies, waits for them, and re-layouts  2.91 us

commit v1 on v0

--- a/solution.py
+++ b/solution.py
@@ -13,43 +13,77 @@
 GROUP = 16
 
 
-PATTERN = "xyzyx"
-SLANT = 0.1
-
+COMPUTE_AT = (0, 19, 25, 12, 4, 1, 3, 2)
+PIECES = (
+    ("gF", (16, 32, 46, 82, 104, 135, 146)),
+    ("A1", (5, 22, 49, 78, 100, 118, 170)),
+    ("A2", (6, 50, 75, 96, 115, 138, 152)),
+    ("gF", (20, 37, 54, 77, 97, 116, 147)),
+    ("A2", (44, 62, 80, 102, 123, 143, 151)),
+    ("A2", (47, 70, 88, 114, 139, 162, 173)),
+    ("A1", (45, 64, 84, 103, 127, 144, 158)),
+    ("A1", (41, 58, 71, 93, 119, 149, 167)),
+    ("gF", (31, 55, 68, 87, 121, 155, 166)),
+    ("gF", (23, 61, 73, 99, 126, 148, 169)),
+    ("A2", (21, 53, 76, 98, 120, 156, 168)),
+    ("A2", (27, 74, 95, 112, 132, 154, 172)),
+    ("A1", (15, 39, 60, 92, 122, 145, 153)),
+    ("gF", (35, 56, 69, 94, 134, 164, 176)),
+    ("A1", (24, 42, 65, 85, 109, 141, 142)),
+    ("y4", (11, 28, 40, 63, 105, 124, 150, 163)),
+    ("gF", (7, 38, 90, 108, 130, 157, 175)),
+    ("A2", (18, 36, 59, 81, 106, 128, 129)),
+    ("gF", (17, 33, 51, 86, 117, 140, 165)),
+    ("A1", (10, 29, 83, 107, 133, 159, 171)),
+    ("A2", (13, 30, 57, 72, 101, 125, 137)),
+    ("gF", (9, 34, 52, 79, 131, 160, 177)),
+    ("x4", (14, 43, 67, 91, 113, 136, 161, 174)),
+    ("A1", (8, 26, 48, 66, 89, 110, 111)),
+)
 
 def stage_orders(rows, cols):
     row_bits = [("row", b) for b in range((rows - 1).bit_length())]
     col_bits = [("col", b) for b in range((cols - 1).bit_length())]
     core, ys, xs, zs = col_bits[0], col_bits[1:], row_bits[0], row_bits[1:]
-    single = lambda bits: [(bit,) for bit in bits]
+    near, far = zs[0], tuple(zs[1:])
+    single = lambda bits: [((bit,), False) for bit in bits]
+    first = ((core,), False)
     return {
-        "x": [(core,), (xs,), *single(ys), tuple(zs)],
-        "y": [(core,), *single(ys), (xs,), tuple(zs)],
-        "X": [(core,), (xs,), *single(ys), *single(zs)],
-        "Y": [(core,), *single(ys), (xs,), *single(zs)],
-        "z": [(core,), *single(zs), (xs, *ys)],
-        "d": [(core,), (xs, *ys), tuple(zs)],
-        "w": [(core,), tuple(zs), (xs, *ys)],
-        "a": [(core,), (xs,), tuple(zs), tuple(ys)],
-        "b": [(core,), tuple(ys), tuple(zs), (xs,)],
+        "x4": [first, ((xs,), False), *single(ys), (tuple(zs), False)],
+        "y4": [first, *single(ys), ((xs,), False), (tuple(zs), False)],
+        "h": [first, *single(zs), ((xs, *ys), False)],
+        "A1": [first, ((xs,), False), ((*ys, near), False), (far, True)],
+        "A2": [first, *single(ys), ((xs, near), False), (far, True)],
+        "gF": [first, ((near,), False), ((xs, *ys), False), (far, True)],
+        "c": [first, ((xs, *ys, near), False), (far, True)],
+        "d": [first, ((xs, *ys), False), (tuple(zs), False)],
+        "dA": [first, ((xs, *ys), False), (tuple(zs), True)],
     }
 
 
 def flips(stage, m):
-    return tuple(bit for j, bit in enumerate(stage) if m >> j & 1)
+    return tuple(bit for j, bit in enumerate(stage[0]) if m >> j & 1)
+
+
+def rounds(order):
+    return 2 * len(order) - (1 if order[-1][1] else 0)
 
 
 def plan(tiles, orders, devices):
-    pieces, events = [], []
-    for first in range(0, tiles, devices):
+    pieces, keyed = [], []
+    for i, first in enumerate(range(0, tiles, devices)):
+        at = COMPUTE_AT[i % len(COMPUTE_AT)]
+        keyed.append((at, -1, "compute", first))
         for array in range(3):
-            pieces.append((array, first, devices, PATTERN[len(pieces) % len(PATTERN)]))
-    keyed = [(SLANT * p - 1, p, "compute") for p in range(0, len(pieces), 3)]
-    for p, piece in enumerate(pieces):
-        keyed += [(SLANT * p + k, p, k) for k in range(2 * len(orders[piece[3]]))]
-    keyed.sort(key=lambda entry: entry[:2])
-    for _, p, k in keyed:
-        events.append(("compute", pieces[p][1]) if k == "compute" else (p, k))
+            name, keys = PIECES[len(pieces) % len(PIECES)]
+            for k in range(rounds(orders[name])):
+                extra = max(0, k + 1 - len(keys))
+                at = max(at, keys[min(k, len(keys) - 1)] + extra)
+                keyed.append((at, len(pieces), k, len(pieces)))
+            at = COMPUTE_AT[i % len(COMPUTE_AT)]
+            pieces.append((array, first, devices, name))
+    keyed.sort(key=lambda entry: entry[:2] + (0 if entry[2] == "compute" else entry[2],))
+    events = [("compute", at) if k == "compute" else (at, k) for _, _, k, at in keyed]
     return pieces, events
 
 
@@ -64,10 +98,10 @@
         lax.fori_loop(0, count // GROUP, step, 0)
 
 
-def kernel(rows, cols, orders, pieces, events, w_hbm, f_hbm, s_hbm, g_hbm, ow, of, os, ins, acc, got, in_sem, send_sem, recv_sem):
+def kernel(rows, cols, orders, pieces, events, w_hbm, f_hbm, s_hbm, g_hbm, ow, of, os, ins, acc, got, wide, in_sem, send_sem, recv_sem):
     me = {"row": lax.axis_index("row"), "col": lax.axis_index("col")}
     outs = (ow, of, os)
-    every_bit = sorted({bit for stage in orders["x"] for bit in stage})
+    every_bit = sorted({bit for stage in orders["x4"] for bit in stage[0]})
     value = {bit: lax.rem(me[bit[0]] // (2 ** bit[1]), 2) for bit in every_bit}
 
     def peer(bits):
@@ -87,7 +121,7 @@
             loads[first, k].start()
 
     used = {piece[3] for piece in pieces}
-    met = sorted({flips(st, m) for o in used for st in orders[o] for m in range(1, 1 << len(st))})
+    met = sorted({flips(st, m) for o in used for st in orders[o] for m in range(1, 1 << len(st[0]))})
     barrier = pltpu.get_barrier_semaphore()
     for bits in met:
         pl.semaphore_signal(barrier, inc=1, device_id=peer(bits), device_id_type=MESH)
@@ -97,12 +131,12 @@
     slots = 0
     for p, (array, first, count, order) in enumerate(pieces):
         off, n = first, count
-        for s, stage in enumerate(orders[order]):
-            n >>= len(stage)
+        for s, (bits, full) in enumerate(orders[order]):
+            n = n if full else n >> len(bits)
             size[p, s] = n
-            for m in range(1 << len(stage)):
+            for m in range(1 << len(bits)):
                 at = off
-                for j, bit in enumerate(stage):
+                for j, bit in enumerate(() if full else bits):
                     v = value[bit]
                     at = at + (1 - v if m >> j & 1 else v) * (n << j)
                 part[p, s, m] = at
@@ -113,9 +147,10 @@
 
     def reduce_copy(p, s, m):
         array, n = pieces[p][0], size[p, s]
+        land = wide.at[m - 1] if orders[pieces[p][3]][s][1] else got
         return pltpu.make_async_remote_copy(
             src_ref=acc.at[array, pl.ds(part[p, s, m], n)],
-            dst_ref=got.at[array, pl.ds(part[p, s, 0], n)],
+            dst_ref=land.at[array, pl.ds(part[p, s, 0], n)],
             send_sem=send_sem.at[slot[p, s, m]],
             recv_sem=recv_sem.at[slot[p, s, m]],
             device_id=peer(flips(orders[pieces[p][3]][s], m)),
@@ -134,7 +169,7 @@
         )
 
     def others(p, s):
-        return range(1, 1 << len(orders[pieces[p][3]][s]))
+        return range(1, 1 << len(orders[pieces[p][3]][s][0]))
 
     copies = []
 
@@ -147,7 +182,8 @@
         shift = at - part[p, s, 0]
         value = acc[array, pl.ds(at, n)]
         for m in others(p, s):
-            value = value + got[array, pl.ds(part[p, s, m] + shift, n)]
+            land = wide.at[m - 1] if orders[pieces[p][3]][s][1] else got
+            value = value + land[array, pl.ds(part[p, s, m] + shift, n)]
         return value
 
     def add(p, s, at, n):
@@ -185,26 +221,43 @@
                     for m in others(q, 0):
                         go(reduce_copy(q, 0, m))
             continue
-        steps = len(orders[pieces[p][3]])
-        s = k if k < steps else 2 * steps - 1 - k
+        order = orders[pieces[p][3]]
+        steps, full = len(order), order[-1][1]
+        s = k if k < steps else 2 * steps - 1 - full - k
         for m in others(p, s):
             (reduce_copy if k < steps else gather_copy)(p, s, m).wait_recv()
         if k + 1 < steps:
             n = size[p, s + 1]
-            for m in others(p, s + 1):
-                add(p, s, part[p, s + 1, m], n)
-                go(reduce_copy(p, s + 1, m))
-            add(p, s, part[p, s + 1, 0], n)
-        elif k + 1 == steps:
-            at, n = part[p, s, 0], size[p, s]
-            outs[pieces[p][0]][pl.ds(at, n)] = total(p, s, at, n) * scale
-            for m in others(p, s):
-                go(gather_copy(p, s, m))
-        elif s > 0:
-            for m in others(p, s - 1):
-                go(gather_copy(p, s - 1, m))
+            if not order[s + 1][1]:
+                for m in others(p, s + 1):
+                    add(p, s, part[p, s + 1, m], n)
+                    go(reduce_copy(p, s + 1, m))
+                add(p, s, part[p, s + 1, 0], n)
+            else:
+                add(p, s, part[p, s + 1, 0], n)
+                for m in others(p, s + 1):
+                    go(reduce_copy(p, s + 1, m))
+        else:
+            if k + 1 == steps:
+                at, n = part[p, s, 0], size[p, s]
+                outs[pieces[p][0]][pl.ds(at, n)] = total(p, s, at, n) * scale
+            s = 2 * steps - 2 - full - k
+            if s >= 0:
+                for m in others(p, s):
+                    go(gather_copy(p, s, m))
     for copy in copies:
         copy.wait_send()
+
+
+def store(a, b, c, out_a, out_b, out_c, sem):
+    copies = [
+        pltpu.make_async_copy(src, dst, sem.at[i])
+        for i, (src, dst) in enumerate(((a, out_a), (b, out_b), (c, out_c)))
+    ]
+    for copy in copies:
+        copy.start()
+    for copy in copies:
+        copy.wait()
 
 
 def as_tiles(x):
@@ -225,7 +278,8 @@
         tiles = shape[0] * shape[1] // 1024
         orders = stage_orders(rows, cols)
         pieces, events = plan(tiles, orders, rows * cols)
-        slots = sum(2 * ((1 << len(stage)) - 1) for piece in pieces for stage in orders[piece[3]])
+        slots = sum(2 * ((1 << len(st[0])) - 1) for piece in pieces for st in orders[piece[3]])
+        most = max([len(st[0]) for piece in pieces for st in orders[piece[3]] if st[1]], default=1)
         spans = len({piece[1] for piece in pieces})
         result = pl.pallas_call(
             functools.partial(kernel, rows, cols, orders, pieces, events),
@@ -236,6 +290,7 @@
                 pltpu.VMEM((4, tiles, 8, 128), jnp.float32),
                 pltpu.VMEM((3, tiles, 8, 128), jnp.float32),
                 pltpu.VMEM((3, tiles, 8, 128), jnp.float32),
+                pltpu.VMEM(((1 << most) - 1, 3, tiles, 8, 128), jnp.float32),
                 pltpu.SemaphoreType.DMA((4, spans)),
                 pltpu.SemaphoreType.DMA((slots,)),
                 pltpu.SemaphoreType.DMA((slots,)),
@@ -244,6 +299,13 @@
                 collective_id=0, has_side_effects=True, vmem_limit_bytes=48 * 1024 * 1024
             ),
         )(*(pltpu.with_memory_space_constraint(as_tiles(x[0, 0]), pltpu.HBM) for x in arrays))
+        result = pl.pallas_call(
+            store,
+            out_shape=(jax.ShapeDtypeStruct((tiles, 8, 128), jnp.float32),) * 3,
+            in_specs=[pl.BlockSpec(memory_space=pltpu.VMEM)] * 3,
+            out_specs=(pl.BlockSpec(memory_space=pltpu.HBM),) * 3,
+            scratch_shapes=[pltpu.SemaphoreType.DMA((3,))],
+        )(*(pltpu.with_memory_space_constraint(x, pltpu.VMEM) for x in result))
         return tuple(from_tiles(x, shape) for x in result)
 
     in_specs = (P("row", "col", None, None),) * 4

time: 50.4 us -> 44.6 us (0.88)
  local copies, waits for them, and re-layouts: 2.91 us -> 0 us
  Pallas kernels: 46.4 us -> 43.6 us
    pallas_call x1, Pallas kernels: 46.4 us -> 42 us  [on_device(): pl.pallas_call(functools.partial(kernel, rows, cols, orders, pieces, even...]
    unnamed x3 -> x0, local copies, waits for them, and re-layouts: 2.91 us -> none
    pallas_call x0 -> x1, Pallas kernels: none -> 1.69 us  [on_device(): pl.pallas_call(store, out_shape=(jax.ShapeDtypeStruct((tiles, 8, 128), jn...]
where the time goes in v1:
time: 44.6 us; the launch traced here: 44.3 us
  Pallas kernels  43.6 us (98%)
  between operations  0.64 us (1%)
    pallas_call x1, Pallas kernels, on_device(): pl.pallas_call(functools.partial(kernel, rows, cols, orders, pieces, even...  42 us
    pallas_call x1, Pallas kernels, on_device(): pl.pallas_call(store, out_shape=(jax.ShapeDtypeStruct((tiles, 8, 128), jn...  1.69 us

profile of v1, /device:TPU:0, one launch (start us, length us, event | category | flops | bytes accessed | tf_op | source)
XLA Modules:
  0.0 44.3 jit_solution(8359894484579567772)
XLA Ops:
  0.6 42.0 %shard_map.67 = (f32[256,8,128]{2,1,0:T(8,128)S(1)}, f32[256,8,128]{2,1,0:T(8,128)S(1)}, f32[256,8,128]{2,1,0:T(8,128)S(1)}) custom-call(f32[256,8,128]{2,1,0:T(8,128)} %bitcast.35, f32[256,8,128]{2,1,0:T(8,128)} %bitcast.36, f32[256,8,128]{2,1,0:T(8,128)} %bitcast.37, f32[256,8,128]{2,1,0:T(8,128)} %bitcast.38), custom_call_target="tpu_custom_call" | custom-call | tf_op jit(solution)/shard_map/pallas_call | solution.py:284
  42.6 1.7 %shard_map.68 = (f32[256,8,128]{2,1,0:T(8,128)}, f32[256,8,128]{2,1,0:T(8,128)}, f32[256,8,128]{2,1,0:T(8,128)}) custom-call(f32[256,8,128]{2,1,0:T(8,128)S(1)} %get-tuple-element.9.a, f32[256,8,128]{2,1,0:T(8,128)S(1)} %get-tuple-element.10.b, f32[256,8,128]{2,1,0:T(8,128)S(1)} %get-tuple-element.11.c), custom_call_target="tpu_custom_call" | custom-call | tf_op jit(solution)/shard_map/pallas_call | solution.py:302

commit v2 on v1

--- a/solution.py
+++ b/solution.py
@@ -98,7 +98,7 @@
         lax.fori_loop(0, count // GROUP, step, 0)
 
 
-def kernel(rows, cols, orders, pieces, events, w_hbm, f_hbm, s_hbm, g_hbm, ow, of, os, ins, acc, got, wide, in_sem, send_sem, recv_sem):
+def kernel(rows, cols, orders, pieces, events, w_hbm, f_hbm, s_hbm, g_hbm, ow, of, os, ins, acc, got, wide, sent, in_sem, send_sem, recv_sem):
     me = {"row": lax.axis_index("row"), "col": lax.axis_index("col")}
     outs = (ow, of, os)
     every_bit = sorted({bit for stage in orders["x4"] for bit in stage[0]})
@@ -112,13 +112,14 @@
 
     spans = sorted({(first, count) for _, first, count, _ in pieces})
     counts = dict(spans)
-    loads = {}
+    loaded = {}
     for i, (first, count) in enumerate(spans):
         for k, src in enumerate((w_hbm, f_hbm, s_hbm, g_hbm)):
-            loads[first, k] = pltpu.make_async_copy(
-                src.at[pl.ds(first, count)], ins.at[k, pl.ds(first, count)], in_sem.at[k, i]
-            )
-            loads[first, k].start()
+            pltpu.make_async_copy(
+                src.at[pl.ds(first, count)], ins.at[k, pl.ds(first, count)], in_sem.at[i]
+            ).start()
+        here = ins.at[:, pl.ds(first, count)]
+        loaded[first] = pltpu.make_async_copy(here, here, in_sem.at[i])
 
     used = {piece[3] for piece in pieces}
     met = sorted({flips(st, m) for o in used for st in orders[o] for m in range(1, 1 << len(st[0]))})
@@ -140,10 +141,9 @@
                     v = value[bit]
                     at = at + (1 - v if m >> j & 1 else v) * (n << j)
                 part[p, s, m] = at
-                if m:
-                    slot[p, s, m] = slots
-                    slots += 2
             off = part[p, s, 0]
+            slot[p, s] = slots
+            slots += 1 if full else 2
 
     def reduce_copy(p, s, m):
         array, n = pieces[p][0], size[p, s]
@@ -151,8 +151,8 @@
         return pltpu.make_async_remote_copy(
             src_ref=acc.at[array, pl.ds(part[p, s, m], n)],
             dst_ref=land.at[array, pl.ds(part[p, s, 0], n)],
-            send_sem=send_sem.at[slot[p, s, m]],
-            recv_sem=recv_sem.at[slot[p, s, m]],
+            send_sem=send_sem.at[0],
+            recv_sem=recv_sem.at[slot[p, s]],
             device_id=peer(flips(orders[pieces[p][3]][s], m)),
             device_id_type=MESH,
         )
@@ -162,8 +162,8 @@
         return pltpu.make_async_remote_copy(
             src_ref=here,
             dst_ref=here,
-            send_sem=send_sem.at[slot[p, s, m] + 1],
-            recv_sem=recv_sem.at[slot[p, s, m] + 1],
+            send_sem=send_sem.at[0],
+            recv_sem=recv_sem.at[slot[p, s] + 1],
             device_id=peer(flips(orders[pieces[p][3]][s], m)),
             device_id_type=MESH,
         )
@@ -171,11 +171,10 @@
     def others(p, s):
         return range(1, 1 << len(orders[pieces[p][3]][s][0]))
 
-    copies = []
-
-    def go(copy):
-        copy.start()
-        copies.append(copy)
+    def arrive(p, s, gather):
+        array, first = pieces[p][:2]
+        here = got.at[array, pl.ds(first, len(others(p, s)) * size[p, s])]
+        pltpu.make_async_copy(here, here, recv_sem.at[slot[p, s] + gather]).wait()
 
     def total(p, s, at, n):
         array = pieces[p][0]
@@ -210,8 +209,7 @@
     scale = 1.0 / (rows * cols)
     for p, k in events:
         if p == "compute":
-            for j in range(4):
-                loads[k, j].wait()
+            loaded[k].wait()
             adamw(k, counts[k])
             if not entered:
                 pl.semaphore_wait(barrier, len(met))
@@ -219,24 +217,23 @@
             for q, piece in enumerate(pieces):
                 if piece[1] == k:
                     for m in others(q, 0):
-                        go(reduce_copy(q, 0, m))
+                        reduce_copy(q, 0, m).start()
             continue
         order = orders[pieces[p][3]]
         steps, full = len(order), order[-1][1]
         s = k if k < steps else 2 * steps - 1 - full - k
-        for m in others(p, s):
-            (reduce_copy if k < steps else gather_copy)(p, s, m).wait_recv()
+        arrive(p, s, 0 if k < steps else 1)
         if k + 1 < steps:
             n = size[p, s + 1]
             if not order[s + 1][1]:
                 for m in others(p, s + 1):
                     add(p, s, part[p, s + 1, m], n)
-                    go(reduce_copy(p, s + 1, m))
+                    reduce_copy(p, s + 1, m).start()
                 add(p, s, part[p, s + 1, 0], n)
             else:
                 add(p, s, part[p, s + 1, 0], n)
                 for m in others(p, s + 1):
-                    go(reduce_copy(p, s + 1, m))
+                    reduce_copy(p, s + 1, m).start()
         else:
             if k + 1 == steps:
                 at, n = part[p, s, 0], size[p, s]
@@ -244,9 +241,8 @@
             s = 2 * steps - 2 - full - k
             if s >= 0:
                 for m in others(p, s):
-                    go(gather_copy(p, s, m))
-    for copy in copies:
-        copy.wait_send()
+                    gather_copy(p, s, m).start()
+    pltpu.make_async_copy(sent, sent, send_sem.at[0]).wait()
 
 
 def store(a, b, c, out_a, out_b, out_c, sem):
@@ -278,7 +274,12 @@
         tiles = shape[0] * shape[1] // 1024
         orders = stage_orders(rows, cols)
         pieces, events = plan(tiles, orders, rows * cols)
-        slots = sum(2 * ((1 << len(st[0])) - 1) for piece in pieces for st in orders[piece[3]])
+        slots, moved = 0, 0
+        for _, _, n, name in pieces:
+            for bits, full in orders[name]:
+                n = n if full else n >> len(bits)
+                slots += 1 if full else 2
+                moved += (1 if full else 2) * ((1 << len(bits)) - 1) * n
         most = max([len(st[0]) for piece in pieces for st in orders[piece[3]] if st[1]], default=1)
         spans = len({piece[1] for piece in pieces})
         result = pl.pallas_call(
@@ -291,8 +292,9 @@
                 pltpu.VMEM((3, tiles, 8, 128), jnp.float32),
                 pltpu.VMEM((3, tiles, 8, 128), jnp.float32),
                 pltpu.VMEM(((1 << most) - 1, 3, tiles, 8, 128), jnp.float32),
-                pltpu.SemaphoreType.DMA((4, spans)),
-                pltpu.SemaphoreType.DMA((slots,)),
+                pltpu.VMEM((moved, 8, 128), jnp.float32),
+                pltpu.SemaphoreType.DMA((spans,)),
+                pltpu.SemaphoreType.DMA((1,)),
                 pltpu.SemaphoreType.DMA((slots,)),
             ],
             compiler_params=pltpu.CompilerParams(

time: 44.6 us -> 40.4 us (0.906)
  Pallas kernels: 43.6 us -> 39.6 us
    pallas_call x1, Pallas kernels: 42 us -> 38 us  [on_device(): pl.pallas_call(functools.partial(kernel, rows, cols, orders, pieces, even...]
where the time goes in v2:
time: 40.4 us; the launch traced here: 40.3 us
  Pallas kernels  39.6 us (98%)
  between operations  0.64 us (2%)
    pallas_call x1, Pallas kernels, on_device(): pl.pallas_call(functools.partial(kernel, rows, cols, orders, pieces, even...  38 us
    pallas_call x1, Pallas kernels, on_device(): pl.pallas_call(store, out_shape=(jax.ShapeDtypeStruct((tiles, 8, 128), jn...  1.69 us

profile of v2, /device:TPU:0, one launch (start us, length us, event | category | flops | bytes accessed | tf_op | source)
XLA Modules:
  0.0 40.3 jit_solution(7647418994980248778)
XLA Ops:
  0.6 38.0 %shard_map.67 = (f32[256,8,128]{2,1,0:T(8,128)S(1)}, f32[256,8,128]{2,1,0:T(8,128)S(1)}, f32[256,8,128]{2,1,0:T(8,128)S(1)}) custom-call(f32[256,8,128]{2,1,0:T(8,128)} %bitcast.35, f32[256,8,128]{2,1,0:T(8,128)} %bitcast.36, f32[256,8,128]{2,1,0:T(8,128)} %bitcast.37, f32[256,8,128]{2,1,0:T(8,128)} %bitcast.38), custom_call_target="tpu_custom_call" | custom-call | tf_op jit(solution)/shard_map/pallas_call | solution.py:285
  38.6 1.7 %shard_map.68 = (f32[256,8,128]{2,1,0:T(8,128)}, f32[256,8,128]{2,1,0:T(8,128)}, f32[256,8,128]{2,1,0:T(8,128)}) custom-call(f32[256,8,128]{2,1,0:T(8,128)S(1)} %get-tuple-element.9.a, f32[256,8,128]{2,1,0:T(8,128)S(1)} %get-tuple-element.10.b, f32[256,8,128]{2,1,0:T(8,128)S(1)} %get-tuple-element.11.c), custom_call_target="tpu_custom_call" | custom-call | tf_op jit(solution)/shard_map/pallas_call | solution.py:304

commit v3 on v2

--- a/solution.py
+++ b/solution.py
@@ -13,6 +13,7 @@
 GROUP = 16
 
 
+COARSE = 1
 COMPUTE_AT = (0, 19, 25, 12, 4, 1, 3, 2)
 PIECES = (
     ("gF", (16, 32, 46, 82, 104, 135, 146)),
@@ -55,6 +56,12 @@
         "A1": [first, ((xs,), False), ((*ys, near), False), (far, True)],
         "A2": [first, *single(ys), ((xs, near), False), (far, True)],
         "gF": [first, ((near,), False), ((xs, *ys), False), (far, True)],
+        "x1": [first, ((xs,), False), *single(ys), ((near,), False), (far, True)],
+        "y1": [first, *single(ys), ((xs,), False), ((near,), False), (far, True)],
+        "x2": [first, ((xs,), False), ((near,), False), *single(ys), (far, True)],
+        "y2": [first, *single(ys), ((near,), False), ((xs,), False), (far, True)],
+        "ux": [first, ((near,), False), ((xs,), False), *single(ys), (far, True)],
+        "uy": [first, ((near,), False), *single(ys), ((xs,), False), (far, True)],
         "c": [first, ((xs, *ys, near), False), (far, True)],
         "d": [first, ((xs, *ys), False), (tuple(zs), False)],
         "dA": [first, ((xs, *ys), False), (tuple(zs), True)],
@@ -71,7 +78,9 @@
 
 def plan(tiles, orders, devices):
     pieces, keyed = [], []
-    for i, first in enumerate(range(0, tiles, devices)):
+    shared = min(len(order[-1][0]) if order[-1][1] else 0 for order in (orders[name] for name, _ in PIECES))
+    count = COARSE * devices >> shared
+    for i, first in enumerate(range(0, tiles, count)):
         at = COMPUTE_AT[i % len(COMPUTE_AT)]
         keyed.append((at, -1, "compute", first))
         for array in range(3):
@@ -81,10 +90,41 @@
                 at = max(at, keys[min(k, len(keys) - 1)] + extra)
                 keyed.append((at, len(pieces), k, len(pieces)))
             at = COMPUTE_AT[i % len(COMPUTE_AT)]
-            pieces.append((array, first, devices, name))
+            pieces.append((array, first, count, name))
     keyed.sort(key=lambda entry: entry[:2] + (0 if entry[2] == "compute" else entry[2],))
     events = [("compute", at) if k == "compute" else (at, k) for _, _, k, at in keyed]
     return pieces, events
+
+
+def receivers(pieces, events, orders):
+    at = {event: i for i, event in enumerate(events)}
+    exchanges = []
+    for p, (_, first, _, name) in enumerate(pieces):
+        order = orders[name]
+        last = rounds(order)
+        for s, stage in enumerate(order):
+            met = [flips(stage, m) for m in range(1, 1 << len(stage[0]))]
+            sent = at["compute", first] if s == 0 else at[p, s - 1]
+            exchanges.append((sent, at[p, s], p, s, 0, met))
+            if not stage[1]:
+                exchanges.append((at[p, last - 2 - s], at[p, last - 1 - s], p, s, 1, met))
+    heard = {}
+    for sent, waited, _, _, _, met in exchanges:
+        for bits in met:
+            row = heard.setdefault(bits, [len(events)] * (len(events) + 1))
+            row[sent] = min(row[sent], waited)
+    for row in heard.values():
+        for i in reversed(range(len(events))):
+            row[i] = min(row[i], row[i + 1])
+    index, ends = {}, []
+    for sent, waited, p, s, gather, met in sorted(exchanges, key=lambda e: e[:5]):
+        free = [
+            (end, j) for j, end in enumerate(ends) if all(heard[bits][end] <= sent for bits in met)
+        ]
+        j = max(free)[1] if free else len(ends)
+        ends[j:j + 1] = [waited]
+        index[p, s, gather] = j
+    return index, len(ends)
 
 
 def for_groups(count, body):
@@ -98,7 +138,7 @@
         lax.fori_loop(0, count // GROUP, step, 0)
 
 
-def kernel(rows, cols, orders, pieces, events, w_hbm, f_hbm, s_hbm, g_hbm, ow, of, os, ins, acc, got, wide, sent, in_sem, send_sem, recv_sem):
+def kernel(rows, cols, orders, pieces, events, index, w_hbm, f_hbm, s_hbm, g_hbm, ow, of, os, ins, acc, got, wide, sent, in_sem, send_sem, recv_sem):
     me = {"row": lax.axis_index("row"), "col": lax.axis_index("col")}
     outs = (ow, of, os)
     every_bit = sorted({bit for stage in orders["x4"] for bit in stage[0]})
@@ -128,8 +168,7 @@
         pl.semaphore_signal(barrier, inc=1, device_id=peer(bits), device_id_type=MESH)
     entered = []
 
-    part, size, slot = {}, {}, {}
-    slots = 0
+    part, size = {}, {}
     for p, (array, first, count, order) in enumerate(pieces):
         off, n = first, count
         for s, (bits, full) in enumerate(orders[order]):
@@ -142,8 +181,6 @@
                     at = at + (1 - v if m >> j & 1 else v) * (n << j)
                 part[p, s, m] = at
             off = part[p, s, 0]
-            slot[p, s] = slots
-            slots += 1 if full else 2
 
     def reduce_copy(p, s, m):
         array, n = pieces[p][0], size[p, s]
@@ -152,7 +189,7 @@
             src_ref=acc.at[array, pl.ds(part[p, s, m], n)],
             dst_ref=land.at[array, pl.ds(part[p, s, 0], n)],
             send_sem=send_sem.at[0],
-            recv_sem=recv_sem.at[slot[p, s]],
+            recv_sem=recv_sem.at[index[p, s, 0]],
             device_id=peer(flips(orders[pieces[p][3]][s], m)),
             device_id_type=MESH,
         )
@@ -163,7 +200,7 @@
             src_ref=here,
             dst_ref=here,
             send_sem=send_sem.at[0],
-            recv_sem=recv_sem.at[slot[p, s] + 1],
+            recv_sem=recv_sem.at[index[p, s, 1]],
             device_id=peer(flips(orders[pieces[p][3]][s], m)),
             device_id_type=MESH,
         )
@@ -174,7 +211,7 @@
     def arrive(p, s, gather):
         array, first = pieces[p][:2]
         here = got.at[array, pl.ds(first, len(others(p, s)) * size[p, s])]
-        pltpu.make_async_copy(here, here, recv_sem.at[slot[p, s] + gather]).wait()
+        pltpu.make_async_copy(here, here, recv_sem.at[index[p, s, gather]]).wait()
 
     def total(p, s, at, n):
         array = pieces[p][0]
@@ -274,16 +311,16 @@
         tiles = shape[0] * shape[1] // 1024
         orders = stage_orders(rows, cols)
         pieces, events = plan(tiles, orders, rows * cols)
-        slots, moved = 0, 0
+        index, slots = receivers(pieces, events, orders)
+        moved = 0
         for _, _, n, name in pieces:
             for bits, full in orders[name]:
                 n = n if full else n >> len(bits)
-                slots += 1 if full else 2
                 moved += (1 if full else 2) * ((1 << len(bits)) - 1) * n
         most = max([len(st[0]) for piece in pieces for st in orders[piece[3]] if st[1]], default=1)
         spans = len({piece[1] for piece in pieces})
         result = pl.pallas_call(
-            functools.partial(kernel, rows, cols, orders, pieces, events),
+            functools.partial(kernel, rows, cols, orders, pieces, events, index),
             out_shape=(pltpu.VMEM((tiles, 8, 128), jnp.float32),) * 3,
             in_specs=[pl.BlockSpec(memory_space=pltpu.HBM)] * 4,
             out_specs=(pl.BlockSpec(memory_space=pltpu.VMEM),) * 3,

time: 40.4 us -> 39.5 us (0.978)
  Pallas kernels: 39.6 us -> 38.7 us
    pallas_call x1, Pallas kernels: 38 us -> 37 us  [on_device(): pl.pallas_call(functools.partial(kernel, rows, cols, orders, pieces, even...]
where the time goes in v3:
time: 39.5 us; the launch traced here: 39.3 us
  Pallas kernels  38.7 us (98%)
  between operations  0.64 us (2%)
    pallas_call x1, Pallas kernels, on_device(): pl.pallas_call(functools.partial(kernel, rows, cols, orders, pieces, even...  37 us
    pallas_call x1, Pallas kernels, on_device(): pl.pallas_call(store, out_shape=(jax.ShapeDtypeStruct((tiles, 8, 128), jn...  1.69 us

profile of v3, /device:TPU:0, one launch (start us, length us, event | category | flops | bytes accessed | tf_op | source)
XLA Modules:
  0.0 39.3 jit_solution(2076903454580677217)
XLA Ops:
  0.6 37.0 %shard_map.67 = (f32[256,8,128]{2,1,0:T(8,128)S(1)}, f32[256,8,128]{2,1,0:T(8,128)S(1)}, f32[256,8,128]{2,1,0:T(8,128)S(1)}) custom-call(f32[256,8,128]{2,1,0:T(8,128)} %bitcast.35, f32[256,8,128]{2,1,0:T(8,128)} %bitcast.36, f32[256,8,128]{2,1,0:T(8,128)} %bitcast.37, f32[256,8,128]{2,1,0:T(8,128)} %bitcast.38), custom_call_target="tpu_custom_call" | custom-call | tf_op jit(solution)/shard_map/pallas_call | solution.py:322
  37.6 1.7 %shard_map.68 = (f32[256,8,128]{2,1,0:T(8,128)}, f32[256,8,128]{2,1,0:T(8,128)}, f32[256,8,128]{2,1,0:T(8,128)}) custom-call(f32[256,8,128]{2,1,0:T(8,128)S(1)} %get-tuple-element.9.a, f32[256,8,128]{2,1,0:T(8,128)S(1)} %get-tuple-element.10.b, f32[256,8,128]{2,1,0:T(8,128)S(1)} %get-tuple-element.11.c), custom_call_target="tpu_custom_call" | custom-call | tf_op jit(solution)/shard_map/pallas_call | solution.py:341

commit v4 on v3

--- a/solution.py
+++ b/solution.py
@@ -14,32 +14,32 @@
 
 
 COARSE = 1
-COMPUTE_AT = (0, 19, 25, 12, 4, 1, 3, 2)
+COMPUTE_AT = (0, 14, 6, 1, 2, 3, 8, 19)
 PIECES = (
-    ("gF", (16, 32, 46, 82, 104, 135, 146)),
-    ("A1", (5, 22, 49, 78, 100, 118, 170)),
-    ("A2", (6, 50, 75, 96, 115, 138, 152)),
-    ("gF", (20, 37, 54, 77, 97, 116, 147)),
-    ("A2", (44, 62, 80, 102, 123, 143, 151)),
-    ("A2", (47, 70, 88, 114, 139, 162, 173)),
-    ("A1", (45, 64, 84, 103, 127, 144, 158)),
-    ("A1", (41, 58, 71, 93, 119, 149, 167)),
-    ("gF", (31, 55, 68, 87, 121, 155, 166)),
-    ("gF", (23, 61, 73, 99, 126, 148, 169)),
-    ("A2", (21, 53, 76, 98, 120, 156, 168)),
-    ("A2", (27, 74, 95, 112, 132, 154, 172)),
-    ("A1", (15, 39, 60, 92, 122, 145, 153)),
-    ("gF", (35, 56, 69, 94, 134, 164, 176)),
-    ("A1", (24, 42, 65, 85, 109, 141, 142)),
-    ("y4", (11, 28, 40, 63, 105, 124, 150, 163)),
-    ("gF", (7, 38, 90, 108, 130, 157, 175)),
-    ("A2", (18, 36, 59, 81, 106, 128, 129)),
-    ("gF", (17, 33, 51, 86, 117, 140, 165)),
-    ("A1", (10, 29, 83, 107, 133, 159, 171)),
-    ("A2", (13, 30, 57, 72, 101, 125, 137)),
-    ("gF", (9, 34, 52, 79, 131, 160, 177)),
-    ("x4", (14, 43, 67, 91, 113, 136, 161, 174)),
-    ("A1", (8, 26, 48, 66, 89, 110, 111)),
+    ("y1", (4, 22, 42, 61, 79, 96, 115, 140, 159)),
+    ("d", (5, 36, 63, 84, 102, 127)),
+    ("A2", (7, 24, 49, 76, 100, 126, 166)),
+    ("A2", (46, 64, 82, 103, 130, 145, 172)),
+    ("gF", (16, 33, 58, 80, 104, 136, 165)),
+    ("d", (15, 34, 54, 77, 111, 112)),
+    ("gF", (41, 62, 87, 108, 131, 153, 163)),
+    ("gF", (29, 57, 75, 95, 119, 149, 157)),
+    ("y4", (23, 50, 66, 92, 113, 134, 148, 160)),
+    ("gF", (9, 26, 44, 67, 105, 125, 133)),
+    ("gF", (12, 31, 48, 74, 98, 116, 150)),
+    ("gF", (35, 60, 88, 109, 138, 155, 169)),
+    ("gF", (13, 45, 73, 93, 121, 143, 161)),
+    ("A1", (10, 25, 43, 71, 101, 122, 123)),
+    ("d", (11, 30, 52, 90, 139, 144)),
+    ("A2", (28, 47, 83, 110, 135, 156, 174)),
+    ("A1", (38, 59, 78, 99, 120, 146, 168)),
+    ("d", (32, 56, 81, 106, 128, 173)),
+    ("d", (17, 37, 86, 118, 142, 170)),
+    ("uy", (18, 39, 55, 70, 91, 107, 129, 141, 167)),
+    ("A1", (27, 68, 94, 114, 137, 154, 164)),
+    ("d", (53, 72, 97, 124, 152, 171)),
+    ("gF", (20, 40, 65, 85, 117, 151, 158)),
+    ("A1", (21, 51, 69, 89, 132, 147, 162)),
 )
 
 def stage_orders(rows, cols):

time: 39.5 us -> 38.8 us (0.982)
  Pallas kernels: 38.7 us -> 38 us
    pallas_call x1, Pallas kernels: 37 us -> 36.3 us  [on_device(): pl.pallas_call(functools.partial(kernel, rows, cols, orders, pieces, even...]
where the time goes in v4:
time: 38.8 us; the launch traced here: 38.7 us
  Pallas kernels  38 us (98%)
  between operations  0.64 us (2%)
    pallas_call x1, Pallas kernels, on_device(): pl.pallas_call(functools.partial(kernel, rows, cols, orders, pieces, even...  36.3 us
    pallas_call x1, Pallas kernels, on_device(): pl.pallas_call(store, out_shape=(jax.ShapeDtypeStruct((tiles, 8, 128), jn...  1.69 us

profile of v4, /device:TPU:0, one launch (start us, length us, event | category | flops | bytes accessed | tf_op | source)
XLA Modules:
  0.0 38.7 jit_solution(9826477115371393299)
XLA Ops:
  0.6 36.3 %shard_map.67 = (f32[256,8,128]{2,1,0:T(8,128)S(1)}, f32[256,8,128]{2,1,0:T(8,128)S(1)}, f32[256,8,128]{2,1,0:T(8,128)S(1)}) custom-call(f32[256,8,128]{2,1,0:T(8,128)} %bitcast.35, f32[256,8,128]{2,1,0:T(8,128)} %bitcast.36, f32[256,8,128]{2,1,0:T(8,128)} %bitcast.37, f32[256,8,128]{2,1,0:T(8,128)} %bitcast.38), custom_call_target="tpu_custom_call" | custom-call | tf_op jit(solution)/shard_map/pallas_call | solution.py:322
  37.0 1.7 %shard_map.68 = (f32[256,8,128]{2,1,0:T(8,128)}, f32[256,8,128]{2,1,0:T(8,128)}, f32[256,8,128]{2,1,0:T(8,128)}) custom-call(f32[256,8,128]{2,1,0:T(8,128)S(1)} %get-tuple-element.9.a, f32[256,8,128]{2,1,0:T(8,128)S(1)} %get-tuple-element.10.b, f32[256,8,128]{2,1,0:T(8,128)S(1)} %get-tuple-element.11.c), custom_call_target="tpu_custom_call" | custom-call | tf_op jit(solution)/shard_map/pallas_call | solution.py:341

commit v5 on v4

--- a/solution.py
+++ b/solution.py
@@ -14,32 +14,32 @@
 
 
 COARSE = 1
-COMPUTE_AT = (0, 14, 6, 1, 2, 3, 8, 19)
+COMPUTE_AT = (0, 10, 2, 1, 5, 6, 3, 8)
 PIECES = (
-    ("y1", (4, 22, 42, 61, 79, 96, 115, 140, 159)),
-    ("d", (5, 36, 63, 84, 102, 127)),
-    ("A2", (7, 24, 49, 76, 100, 126, 166)),
-    ("A2", (46, 64, 82, 103, 130, 145, 172)),
-    ("gF", (16, 33, 58, 80, 104, 136, 165)),
-    ("d", (15, 34, 54, 77, 111, 112)),
-    ("gF", (41, 62, 87, 108, 131, 153, 163)),
-    ("gF", (29, 57, 75, 95, 119, 149, 157)),
-    ("y4", (23, 50, 66, 92, 113, 134, 148, 160)),
-    ("gF", (9, 26, 44, 67, 105, 125, 133)),
-    ("gF", (12, 31, 48, 74, 98, 116, 150)),
-    ("gF", (35, 60, 88, 109, 138, 155, 169)),
-    ("gF", (13, 45, 73, 93, 121, 143, 161)),
-    ("A1", (10, 25, 43, 71, 101, 122, 123)),
-    ("d", (11, 30, 52, 90, 139, 144)),
-    ("A2", (28, 47, 83, 110, 135, 156, 174)),
-    ("A1", (38, 59, 78, 99, 120, 146, 168)),
-    ("d", (32, 56, 81, 106, 128, 173)),
-    ("d", (17, 37, 86, 118, 142, 170)),
-    ("uy", (18, 39, 55, 70, 91, 107, 129, 141, 167)),
-    ("A1", (27, 68, 94, 114, 137, 154, 164)),
-    ("d", (53, 72, 97, 124, 152, 171)),
-    ("gF", (20, 40, 65, 85, 117, 151, 158)),
-    ("A1", (21, 51, 69, 89, 132, 147, 162)),
+    ("d", (4, 24, 62, 86, 114, 143)),
+    ("gF", (7, 21, 39, 61, 80, 104, 121)),
+    ("d", (11, 25, 42, 70, 90, 107)),
+    ("d", (51, 76, 96, 136, 161, 169)),
+    ("A2", (40, 63, 83, 111, 132, 150, 162)),
+    ("d", (34, 54, 88, 124, 155, 168)),
+    ("gF", (14, 28, 46, 75, 101, 125, 139)),
+    ("gF", (17, 32, 49, 69, 87, 113, 135)),
+    ("A1", (45, 67, 89, 112, 129, 152, 166)),
+    ("ux", (12, 29, 48, 68, 91, 108, 127, 149, 160)),
+    ("gF", (27, 58, 77, 97, 123, 142, 163)),
+    ("d", (9, 26, 53, 73, 98, 119)),
+    ("A2", (35, 55, 79, 102, 126, 148, 159)),
+    ("A2", (16, 31, 52, 72, 103, 130, 146)),
+    ("d", (18, 36, 57, 82, 100, 106)),
+    ("gF", (22, 47, 74, 94, 116, 138, 157)),
+    ("A1", (37, 59, 85, 109, 128, 141, 153)),
+    ("gF", (30, 60, 81, 105, 131, 154, 165)),
+    ("d", (13, 33, 56, 92, 115, 133)),
+    ("gF", (38, 64, 84, 110, 134, 158, 167)),
+    ("d", (20, 41, 78, 117, 151, 164)),
+    ("gF", (19, 44, 66, 99, 122, 140, 145)),
+    ("A1", (15, 43, 65, 93, 118, 147, 156)),
+    ("A2", (23, 50, 71, 95, 120, 137, 144)),
 )
 
 def stage_orders(rows, cols):
@@ -64,6 +64,7 @@
         "uy": [first, ((near,), False), *single(ys), ((xs,), False), (far, True)],
         "c": [first, ((xs, *ys, near), False), (far, True)],
         "d": [first, ((xs, *ys), False), (tuple(zs), False)],
+        "dR": [first, ((xs, *ys), False), ((near,), True), (far, True)],
         "dA": [first, ((xs, *ys), False), (tuple(zs), True)],
     }
 
@@ -206,7 +207,7 @@
         )
 
     def others(p, s):
-        return range(1, 1 << len(orders[pieces[p][3]][s][0]))
+        return range((1 << len(orders[pieces[p][3]][s][0])) - 1, 0, -1)
 
     def arrive(p, s, gather):
         array, first = pieces[p][:2]

time: 38.8 us -> 38.4 us (0.990)
  Pallas kernels: 38 us -> 37.6 us
    pallas_call x1, Pallas kernels: 36.3 us -> 35.9 us  [on_device(): pl.pallas_call(functools.partial(kernel, rows, cols, orders, pieces, even...]
where the time goes in v5:
time: 38.4 us; the launch traced here: 38.2 us
  Pallas kernels  37.6 us (98%)
  between operations  0.64 us (2%)
    pallas_call x1, Pallas kernels, on_device(): pl.pallas_call(functools.partial(kernel, rows, cols, orders, pieces, even...  35.9 us
    pallas_call x1, Pallas kernels, on_device(): pl.pallas_call(store, out_shape=(jax.ShapeDtypeStruct((tiles, 8, 128), jn...  1.69 us

profile of v5, /device:TPU:0, one launch (start us, length us, event | category | flops | bytes accessed | tf_op | source)
XLA Modules:
  0.0 38.2 jit_solution(8357579510613139244)
XLA Ops:
  0.6 35.9 %shard_map.67 = (f32[256,8,128]{2,1,0:T(8,128)S(1)}, f32[256,8,128]{2,1,0:T(8,128)S(1)}, f32[256,8,128]{2,1,0:T(8,128)S(1)}) custom-call(f32[256,8,128]{2,1,0:T(8,128)} %bitcast.35, f32[256,8,128]{2,1,0:T(8,128)} %bitcast.36, f32[256,8,128]{2,1,0:T(8,128)} %bitcast.37, f32[256,8,128]{2,1,0:T(8,128)} %bitcast.38), custom_call_target="tpu_custom_call" | custom-call | tf_op jit(solution)/shard_map/pallas_call | solution.py:323
  36.5 1.7 %shard_map.68 = (f32[256,8,128]{2,1,0:T(8,128)}, f32[256,8,128]{2,1,0:T(8,128)}, f32[256,8,128]{2,1,0:T(8,128)}) custom-call(f32[256,8,128]{2,1,0:T(8,128)S(1)} %get-tuple-element.9.a, f32[256,8,128]{2,1,0:T(8,128)S(1)} %get-tuple-element.10.b, f32[256,8,128]{2,1,0:T(8,128)S(1)} %get-tuple-element.11.c), custom_call_target="tpu_custom_call" | custom-call | tf_op jit(solution)/shard_map/pallas_call | solution.py:342

commit v6 on v5

--- a/solution.py
+++ b/solution.py
@@ -22,7 +22,7 @@
     ("d", (51, 76, 96, 136, 161, 169)),
     ("A2", (40, 63, 83, 111, 132, 150, 162)),
     ("d", (34, 54, 88, 124, 155, 168)),
-    ("gF", (14, 28, 46, 75, 101, 125, 139)),
+    ("gF", (14, 28, 46, 75, 101, 125, 138)),
     ("gF", (17, 32, 49, 69, 87, 113, 135)),
     ("A1", (45, 67, 89, 112, 129, 152, 166)),
     ("ux", (12, 29, 48, 68, 91, 108, 127, 149, 160)),
@@ -31,7 +31,7 @@
     ("A2", (35, 55, 79, 102, 126, 148, 159)),
     ("A2", (16, 31, 52, 72, 103, 130, 146)),
     ("d", (18, 36, 57, 82, 100, 106)),
-    ("gF", (22, 47, 74, 94, 116, 138, 157)),
+    ("gF", (22, 47, 74, 94, 116, 139, 157)),
     ("A1", (37, 59, 85, 109, 128, 141, 153)),
     ("gF", (30, 60, 81, 105, 131, 154, 165)),
     ("d", (13, 33, 56, 92, 115, 133)),
@@ -67,6 +67,11 @@
         "dR": [first, ((xs, *ys), False), ((near,), True), (far, True)],
         "dA": [first, ((xs, *ys), False), (tuple(zs), True)],
     }
+
+
+def twins(rows, cols):
+    x, y = ("row", 0), ("col", 1)
+    return {x: y, y: x} if (cols - 1).bit_length() == 2 and rows > 1 else {}
 
 
 def flips(stage, m):
@@ -145,10 +150,18 @@
     every_bit = sorted({bit for stage in orders["x4"] for bit in stage[0]})
     value = {bit: lax.rem(me[bit[0]] // (2 ** bit[1]), 2) for bit in every_bit}
 
+    core, twin = value[orders["x4"][0][0][0]], twins(rows, cols)
+    value.update({a: value[a] + core * (value[b] - value[a]) for a, b in twin.items()})
+
     def peer(bits):
         other = dict(me)
         for bit in bits:
-            other[bit[0]] = other[bit[0]] + (1 - 2 * value[bit]) * (2 ** bit[1])
+            step = 1 - 2 * value[bit]
+            if bit in twin:
+                axis, place = twin[bit]
+                other[axis] = other[axis] + core * step * (2 ** place)
+                step = (1 - core) * step
+            other[bit[0]] = other[bit[0]] + step * (2 ** bit[1])
         return other["row"], other["col"]
 
     spans = sorted({(first, count) for _, first, count, _ in pieces})

time: 38.4 us -> 38.3 us (level)
  no operation moved by 1% of the time
where the time goes in v6:
time: 38.3 us; the launch traced here: 38.2 us
  Pallas kernels  37.5 us (98%)
  between operations  0.64 us (2%)
    pallas_call x1, Pallas kernels, on_device(): pl.pallas_call(functools.partial(kernel, rows, cols, orders, pieces, even...  35.8 us
    pallas_call x1, Pallas kernels, on_device(): pl.pallas_call(store, out_shape=(jax.ShapeDtypeStruct((tiles, 8, 128), jn...  1.69 us

profile of v6, /device:TPU:0, one launch (start us, length us, event | category | flops | bytes accessed | tf_op | source)
XLA Modules:
  0.0 38.2 jit_solution(15846854125815779782)
XLA Ops:
  0.6 35.8 %shard_map.67 = (f32[256,8,128]{2,1,0:T(8,128)S(1)}, f32[256,8,128]{2,1,0:T(8,128)S(1)}, f32[256,8,128]{2,1,0:T(8,128)S(1)}) custom-call(f32[256,8,128]{2,1,0:T(8,128)} %bitcast.35, f32[256,8,128]{2,1,0:T(8,128)} %bitcast.36, f32[256,8,128]{2,1,0:T(8,128)} %bitcast.37, f32[256,8,128]{2,1,0:T(8,128)} %bitcast.38), custom_call_target="tpu_custom_call" | custom-call | tf_op jit(solution)/shard_map/pallas_call | solution.py:336
  36.5 1.7 %shard_map.68 = (f32[256,8,128]{2,1,0:T(8,128)}, f32[256,8,128]{2,1,0:T(8,128)}, f32[256,8,128]{2,1,0:T(8,128)}) custom-call(f32[256,8,128]{2,1,0:T(8,128)S(1)} %get-tuple-element.9.a, f32[256,8,128]{2,1,0:T(8,128)S(1)} %get-tuple-element.10.b, f32[256,8,128]{2,1,0:T(8,128)S(1)} %get-tuple-element.11.c), custom_call_target="tpu_custom_call" | custom-call | tf_op jit(solution)/shard_map/pallas_call | solution.py:355

commit v7 on v6

--- a/solution.py
+++ b/solution.py
@@ -104,16 +104,21 @@
 
 def receivers(pieces, events, orders):
     at = {event: i for i, event in enumerate(events)}
-    exchanges = []
+    exchanges, spans = [], {}
     for p, (_, first, _, name) in enumerate(pieces):
         order = orders[name]
         last = rounds(order)
         for s, stage in enumerate(order):
             met = [flips(stage, m) for m in range(1, 1 << len(stage[0]))]
-            sent = at["compute", first] if s == 0 else at[p, s - 1]
-            exchanges.append((sent, at[p, s], p, s, 0, met))
+            if s == 0:
+                spans.setdefault(first, []).append((at[p, 0], p, met))
+                continue
+            exchanges.append((at[p, s - 1], at[p, s], p, s, 0, met))
             if not stage[1]:
                 exchanges.append((at[p, last - 2 - s], at[p, last - 1 - s], p, s, 1, met))
+    for first, members in spans.items():
+        waited, p, met = min(members)
+        exchanges.append((at["compute", first], waited, p, 0, 0, met))
     heard = {}
     for sent, waited, _, _, _, met in exchanges:
         for bits in met:
@@ -130,7 +135,11 @@
         j = max(free)[1] if free else len(ends)
         ends[j:j + 1] = [waited]
         index[p, s, gather] = j
-    return index, len(ends)
+    for members in spans.values():
+        for _, p, _ in members:
+            index[p, 0, 0] = index[min(members)[1], 0, 0]
+            index[p, 0, 1] = len(ends)
+    return index, len(ends) + 1
 
 
 def for_groups(count, body):
@@ -222,8 +231,16 @@
     def others(p, s):
         return range((1 << len(orders[pieces[p][3]][s][0])) - 1, 0, -1)
 
+    arrived = set()
+
     def arrive(p, s, gather):
         array, first = pieces[p][:2]
+        if s == 0:
+            if not gather and first not in arrived:
+                here = got.at[:, pl.ds(first, size[p, 0])]
+                pltpu.make_async_copy(here, here, recv_sem.at[index[p, 0, 0]]).wait()
+                arrived.add(first)
+            return
         here = got.at[array, pl.ds(first, len(others(p, s)) * size[p, s])]
         pltpu.make_async_copy(here, here, recv_sem.at[index[p, s, gather]]).wait()
 
@@ -293,6 +310,8 @@
             if s >= 0:
                 for m in others(p, s):
                     gather_copy(p, s, m).start()
+    half = got.at[:, pl.ds(0, got.shape[1] // 2)]
+    pltpu.make_async_copy(half, half, recv_sem.at[index[0, 0, 1]]).wait()
     pltpu.make_async_copy(sent, sent, send_sem.at[0]).wait()
 
 

time: 38.3 us -> 38.2 us (level)
  no operation moved by 1% of the time
where the time goes in v7:
time: 38.2 us; the launch traced here: 38.1 us
  Pallas kernels  37.4 us (98%)
  between operations  0.64 us (2%)
    pallas_call x1, Pallas kernels, on_device(): pl.pallas_call(functools.partial(kernel, rows, cols, orders, pieces, even...  35.7 us
    pallas_call x1, Pallas kernels, on_device(): pl.pallas_call(store, out_shape=(jax.ShapeDtypeStruct((tiles, 8, 128), jn...  1.69 us

profile of v7, /device:TPU:0, one launch (start us, length us, event | category | flops | bytes accessed | tf_op | source)
XLA Modules:
  0.0 38.1 jit_solution(9254429527702357745)
XLA Ops:
  0.6 35.7 %shard_map.67 = (f32[256,8,128]{2,1,0:T(8,128)S(1)}, f32[256,8,128]{2,1,0:T(8,128)S(1)}, f32[256,8,128]{2,1,0:T(8,128)S(1)}) custom-call(f32[256,8,128]{2,1,0:T(8,128)} %bitcast.35, f32[256,8,128]{2,1,0:T(8,128)} %bitcast.36, f32[256,8,128]{2,1,0:T(8,128)} %bitcast.37, f32[256,8,128]{2,1,0:T(8,128)} %bitcast.38), custom_call_target="tpu_custom_call" | custom-call | tf_op jit(solution)/shard_map/pallas_call | solution.py:355
  36.4 1.7 %shard_map.68 = (f32[256,8,128]{2,1,0:T(8,128)}, f32[256,8,128]{2,1,0:T(8,128)}, f32[256,8,128]{2,1,0:T(8,128)}) custom-call(f32[256,8,128]{2,1,0:T(8,128)S(1)} %get-tuple-element.9.a, f32[256,8,128]{2,1,0:T(8,128)S(1)} %get-tuple-element.10.b, f32[256,8,128]{2,1,0:T(8,128)S(1)} %get-tuple-element.11.c), custom_call_target="tpu_custom_call" | custom-call | tf_op jit(solution)/shard_map/pallas_call | solution.py:374
